TPU v7x, 512 devices: a whole 4x4x16 slice. The times are simulated.
512 devices in a mesh: seq: 16 (over z), head: 32 (over x, y, core).
Axes of the slice: x: 4, y: 4, z: 16, core: 2. Of those that a mesh axis runs over, the one named last changes fastest.
Arguments:
- queries: bfloat16 [16384, 8192], P('seq', 'head'), may hold values from -6 to 6
- keys: bfloat16 [16384, 8192], P('seq', 'head'), may hold values from -1 to 1
- values: bfloat16 [16384, 8192], P('seq', 'head'), may hold values from -40 to 40
- log_decay: float32 [64, 16384], P('head', 'seq'), may hold values from -1 to 0
- gain: float32 [8192], P('head'), may hold values from 0.25 to 1.75
- out_grad: bfloat16 [16384, 8192], P('seq', 'head'), may hold values from -16 to 16
Outputs:
- output: bfloat16 [16384, 8192], P('seq', 'head')
- query_grad: bfloat16 [16384, 8192], P('seq', 'head')
- key_grad: bfloat16 [16384, 8192], P('seq', 'head')
- value_grad: bfloat16 [16384, 8192], P('seq', 'head')
- gain_grad: float32 [8192], P('head')
All inputs are finite; a program needn't handle non-finite values.
Results may differ from a plain program's by a relative error of at most 0.001.
Values sent between devices are 32-bit elements; how exact they have to be, the bound alone decides.
No kernel may reach another device: no remote copies, remote signals or barrier semaphores. Data moves between devices by JAX's collectives and lax.ppermute only.
A program may use at most 64 MiB of HBM per device.

v0:
```python
import jax
import jax.numpy as jnp
from jax import lax
from jax.sharding import PartitionSpec as P

epsilon = 1e-06
highest = lax.Precision.HIGHEST


def passed_along(value, axis, steps):
    count = lax.axis_size(axis)
    initial, last = (max(0, -steps), min(count, count - steps))
    return lax.ppermute(value, axis, [(source, source + steps) for source in range(initial, last)])


def to_blocks(matrix, heads_local, block_count, block_rows):
    head_width = matrix.shape[1] // heads_local
    return matrix.reshape(block_count, block_rows, heads_local, head_width).transpose(2, 0, 1, 3)


def from_blocks(blocked):
    heads_local, block_count, block_rows, head_width = blocked.shape
    return blocked.transpose(1, 2, 0, 3).reshape(block_count * block_rows, heads_local * head_width)


def carry_forward(device_decay, device_state):

    def relay_step(iteration, prefix):
        outgoing = jnp.exp(device_decay)[:, None, None] * prefix + device_state
        return passed_along(outgoing, "seq", 1)

    return lax.fori_loop(0, lax.axis_size("seq") - 1, relay_step, jnp.zeros_like(device_state))


def carry_backward(device_decay, device_back):

    def relay_step(iteration, suffix):
        outgoing = jnp.exp(device_decay)[:, None, None] * suffix + device_back
        return passed_along(outgoing, "seq", -1)

    return lax.fori_loop(0, lax.axis_size("seq") - 1, relay_step, jnp.zeros_like(device_back))


def local(queries, keys, values, log_decay, gain, out_grad):
    token_rows, channels = queries.shape
    heads_local = log_decay.shape[0]
    block_rows = min(256, token_rows)
    block_count = token_rows // block_rows
    total_channels = channels * lax.axis_size("head")
    query_narrow = to_blocks(queries, heads_local, block_count, block_rows)
    key_narrow = to_blocks(keys, heads_local, block_count, block_rows)
    query_blocks = query_narrow.astype(jnp.float32)
    key_blocks = key_narrow.astype(jnp.float32)
    value_blocks = to_blocks(values, heads_local, block_count, block_rows).astype(jnp.float32)
    decay_sum = jnp.cumsum(log_decay.reshape(heads_local, block_count, block_rows), axis=2)
    block_total = decay_sum[:, :, -1]
    causal = jnp.arange(block_rows)[:, None] >= jnp.arange(block_rows)[None, :]
    mask_decay = jnp.exp(
        jnp.where(causal, decay_sum[..., :, None] - decay_sum[..., None, :], -1e30)
    )
    from_start = jnp.exp(decay_sum)[..., None]
    to_end = jnp.exp(block_total[..., None] - decay_sum)[..., None]
    scores = (
        jnp.einsum("hnid,hnjd->hnij", query_narrow, key_narrow, preferred_element_type=jnp.float32)
        * mask_decay
    )
    inside = jnp.einsum("hnij,hnjd->hnid", scores, value_blocks, precision=highest)
    own_states = jnp.einsum("hnjd,hnje->hnde", key_blocks * to_end, value_blocks, precision=highest)
    device_decay = jnp.sum(block_total, axis=1)
    device_state = jnp.zeros_like(own_states[:, 0])
    for block_index in range(block_count):
        device_state = (
            jnp.exp(block_total[:, block_index])[:, None, None] * device_state
            + own_states[:, block_index]
        )
    incoming = carry_forward(device_decay, device_state)
    entering = []
    running = incoming
    for block_index in range(block_count):
        entering.append(running)
        running = (
            jnp.exp(block_total[:, block_index])[:, None, None] * running
            + own_states[:, block_index]
        )
    entering = jnp.stack(entering, axis=1)
    attended = inside + from_start * jnp.einsum(
        "hnid,hnde->hnie", query_blocks, entering, precision=highest
    )
    flattened = from_blocks(attended)
    grad_wide = out_grad.astype(jnp.float32)
    normed_grad = grad_wide * gain
    squares = lax.psum(jnp.sum(flattened * flattened, axis=1), "head")
    inverse = 1.0 / jnp.sqrt(squares / total_channels + epsilon)
    normed = flattened * inverse[:, None]
    projected = lax.psum(jnp.sum(normed_grad * normed, axis=1), "head")
    output = (normed * gain).astype(jnp.bfloat16)
    gain_part = jnp.sum(grad_wide * normed, axis=0)
    flat_grad = (normed_grad - normed * (projected / total_channels)[:, None]) * inverse[:, None]
    attended_grad = to_blocks(flat_grad, heads_local, block_count, block_rows)
    score_grad = (
        jnp.einsum("hnid,hnjd->hnij", attended_grad, value_blocks, precision=highest) * mask_decay
    )
    query_grad = jnp.einsum("hnij,hnjd->hnid", score_grad, key_blocks, precision=highest)
    query_grad = query_grad + from_start * jnp.einsum(
        "hnie,hnde->hnid", attended_grad, entering, precision=highest
    )
    key_grad = jnp.einsum("hnij,hnid->hnjd", score_grad, query_blocks, precision=highest)
    value_grad = jnp.einsum("hnij,hnid->hnjd", scores, attended_grad, precision=highest)
    own_back = jnp.einsum(
        "hnid,hnie->hnde", query_blocks * from_start, attended_grad, precision=highest
    )
    device_back = jnp.zeros_like(device_state)
    for block_index in reversed(range(block_count)):
        device_back = (
            own_back[:, block_index]
            + jnp.exp(block_total[:, block_index])[:, None, None] * device_back
        )
    later_sum = carry_backward(device_decay, device_back)
    leaving = []
    running = later_sum
    for block_index in reversed(range(block_count)):
        leaving.append(running)
        running = (
            own_back[:, block_index] + jnp.exp(block_total[:, block_index])[:, None, None] * running
        )
    leaving = jnp.stack(leaving[::-1], axis=1)
    key_grad = key_grad + to_end * jnp.einsum(
        "hnje,hnde->hnjd", value_blocks, leaving, precision=highest
    )
    value_grad = value_grad + to_end * jnp.einsum(
        "hnjd,hnde->hnje", key_blocks, leaving, precision=highest
    )
    gain_grad = lax.psum(gain_part, "seq")
    return (
        output,
        from_blocks(query_grad).astype(jnp.bfloat16),
        from_blocks(key_grad).astype(jnp.bfloat16),
        from_blocks(value_grad).astype(jnp.bfloat16),
        gain_grad,
    )


def solution(mesh):
    in_specs = (
        P("seq", "head"),
        P("seq", "head"),
        P("seq", "head"),
        P("head", "seq"),
        P("head"),
        P("seq", "head"),
    )
    out_specs = (P("seq", "head"), P("seq", "head"), P("seq", "head"), P("seq", "head"), P("head"))
    return jax.shard_map(local, mesh=mesh, in_specs=in_specs, out_specs=out_specs, check_vma=False)
```

profile of v0, /device:TPU:96, one launch (start us, length us, event | category | flops | bytes accessed | tf_op | source)
XLA Modules:
  0.0 471.4 jit_solution(15646903390274113141)
XLA Ops:
  9.9 125.4 %while.24 = (s32[]{:T(128)}, f32[2,128,128]{2,1,0:T(8,128)S(1)}, f32[2,1,1]{0,2,1:T(1,128)S(1)}, f32[2,128,128]{2,1,0:T(8,128)S(1)}, s32[]{:T(128)}) while((s32[]{:T(128)}, f32[2,128,128]{2,1,0:T(8,128)S(1)}, f32[2,1,1]{0,2,1:T(1,128)S(1)}, f32[2,128,128]{2,1,0:T(8,128)S(1)}, s32[]{:T(128)}) %tuple.63), condition=%wide.region_4.5_spmd, body=%wide.region_3.4_spmd.sunk | while | flops 65538 | bytes 917613 | solution.py:32
  17.8 5.6 %collective-permute-start = (f32[2,128,128]{2,1,0:T(8,128)S(1)}, f32[2,128,128]{2,1,0:T(8,128)S(1)}, u32[]{:S(2)}, u32[]{:S(2)}) collective-permute-start(f32[2,128,128]{2,1,0:T(8,128)S(1)} %multiply_add_fusion.10), channel_id=1, source_target_pairs={{0,32},{32,64},{64,96},{96,128},{128,160},{160,192},{192,224},{224... | collective-permute-start | bytes 393224 | tf_op jit(solution)/shard_map/while/body/eval_jaxpr/ppermute | solution.py:13
  59.6 5.6 %collective-permute-start = (f32[2,128,128]{2,1,0:T(8,128)S(1)}, f32[2,128,128]{2,1,0:T(8,128)S(1)}, u32[]{:S(2)}, u32[]{:S(2)}) collective-permute-start(f32[2,128,128]{2,1,0:T(8,128)S(1)} %multiply_add_fusion.10), channel_id=1, source_target_pairs={{0,32},{32,64},{64,96},{96,128},{128,160},{160,192},{192,224},{224... | collective-permute-start | bytes 393224 | tf_op jit(solution)/shard_map/while/body/eval_jaxpr/ppermute | solution.py:13
  109.8 5.6 %collective-permute-start = (f32[2,128,128]{2,1,0:T(8,128)S(1)}, f32[2,128,128]{2,1,0:T(8,128)S(1)}, u32[]{:S(2)}, u32[]{:S(2)}) collective-permute-start(f32[2,128,128]{2,1,0:T(8,128)S(1)} %multiply_add_fusion.10), channel_id=1, source_target_pairs={{0,32},{32,64},{64,96},{96,128},{128,160},{160,192},{192,224},{224... | collective-permute-start | bytes 393224 | tf_op jit(solution)/shard_map/while/body/eval_jaxpr/ppermute | solution.py:13
  139.9 62.7 %psum.21 = f32[1024]{0:T(1024)S(1)} all-reduce(f32[1024]{0:T(1024)S(1)} %bitcast.231), channel_id=1, replica_groups=mesh['seq'=16,'head'=32] {'head'}, use_global_device_ids=true, to_apply=%region_6.7 | all-reduce | flops 1024 | bytes 8192 | tf_op jit(solution)/shard_map/psum | solution.py:92
  204.7 32.4 %psum.23 = f32[256]{0:T(256)} all-reduce(f32[256]{0:T(256)S(1)} %get-tuple-element.107), channel_id=1, replica_groups=mesh['seq'=16,'head'=32] {'seq'}, use_global_device_ids=true, to_apply=%region_12.13 | all-reduce | flops 256 | bytes 2048 | tf_op jit(solution)/shard_map/psum | solution.py:133
  237.2 62.7 %psum.22 = f32[1024]{0:T(1024)S(1)} all-reduce(f32[1024]{0:T(1024)S(1)} %get-tuple-element.108), channel_id=1, replica_groups=mesh['seq'=16,'head'=32] {'head'}, use_global_device_ids=true, to_apply=%region_8.9 | all-reduce | flops 1024 | bytes 8192 | tf_op jit(solution)/shard_map/psum | solution.py:95
  303.1 6.1 %convolution_bitcast_fusion.4 = f32[4,256,2,128]{3,1,0,2:T(8,128)} fusion(f32[2,4,256,256]{3,2,1,0:T(8,128)} %copy-done, f32[4,256,2,128]{3,2,1,0:T(2,128)S(1)} %reshape.129), kind=kOutput, calls=%fused_computation.11 | convolution fusion | flops 805306368 | bytes 4194304 | tf_op jit(solution)/shard_map/hnij,hnid->hnjd/dot_general | solution.py:108
  310.5 147.5 %while.25 = (s32[]{:T(128)}, f32[2,128,128]{2,1,0:T(8,128)S(1)}, f32[2,1,1]{0,2,1:T(1,128)}, f32[2,128,128]{2,1,0:T(8,128)S(1)}, s32[]{:T(128)}) while((s32[]{:T(128)}, f32[2,128,128]{2,1,0:T(8,128)S(1)}, f32[2,1,1]{0,2,1:T(1,128)}, f32[2,128,128]{2,1,0:T(8,128)S(1)}, s32[]{:T(128)}) %tuple.69), condition=%wide.region_10.11_spmd, body=%wide.region_9.10_spmd.sunk | while | flops 65538 | bytes 917613 | solution.py:41
  314.1 6.6 %collective-permute-done.1 = f32[2,128,128]{2,1,0:T(8,128)S(1)} collective-permute-done((f32[2,128,128]{2,1,0:T(8,128)}, f32[2,128,128]{2,1,0:T(8,128)S(1)}, u32[]{:S(2)}, u32[]{:S(2)}) %collective-permute-start.1) | collective-permute-done | bytes 131104 | tf_op jit(solution)/shard_map/while/body/eval_jaxpr/ppermute | solution.py:13
  324.0 6.4 %collective-permute-done.1 = f32[2,128,128]{2,1,0:T(8,128)S(1)} collective-permute-done((f32[2,128,128]{2,1,0:T(8,128)}, f32[2,128,128]{2,1,0:T(8,128)S(1)}, u32[]{:S(2)}, u32[]{:S(2)}) %collective-permute-start.1) | collective-permute-done | bytes 131104 | tf_op jit(solution)/shard_map/while/body/eval_jaxpr/ppermute | solution.py:13
  333.7 6.4 %collective-permute-done.1 = f32[2,128,128]{2,1,0:T(8,128)S(1)} collective-permute-done((f32[2,128,128]{2,1,0:T(8,128)}, f32[2,128,128]{2,1,0:T(8,128)S(1)}, u32[]{:S(2)}, u32[]{:S(2)}) %collective-permute-start.1) | collective-permute-done | bytes 131104 | tf_op jit(solution)/shard_map/while/body/eval_jaxpr/ppermute | solution.py:13
  343.4 6.4 %collective-permute-done.1 = f32[2,128,128]{2,1,0:T(8,128)S(1)} collective-permute-done((f32[2,128,128]{2,1,0:T(8,128)}, f32[2,128,128]{2,1,0:T(8,128)S(1)}, u32[]{:S(2)}, u32[]{:S(2)}) %collective-permute-start.1) | collective-permute-done | bytes 131104 | tf_op jit(solution)/shard_map/while/body/eval_jaxpr/ppermute | solution.py:13
  353.1 6.4 %collective-permute-done.1 = f32[2,128,128]{2,1,0:T(8,128)S(1)} collective-permute-done((f32[2,128,128]{2,1,0:T(8,128)}, f32[2,128,128]{2,1,0:T(8,128)S(1)}, u32[]{:S(2)}, u32[]{:S(2)}) %collective-permute-start.1) | collective-permute-done | bytes 131104 | tf_op jit(solution)/shard_map/while/body/eval_jaxpr/ppermute | solution.py:13
  362.8 6.4 %collective-permute-done.1 = f32[2,128,128]{2,1,0:T(8,128)S(1)} collective-permute-done((f32[2,128,128]{2,1,0:T(8,128)}, f32[2,128,128]{2,1,0:T(8,128)S(1)}, u32[]{:S(2)}, u32[]{:S(2)}) %collective-permute-start.1) | collective-permute-done | bytes 131104 | tf_op jit(solution)/shard_map/while/body/eval_jaxpr/ppermute | solution.py:13
  372.4 6.9 %collective-permute-done.1 = f32[2,128,128]{2,1,0:T(8,128)S(1)} collective-permute-done((f32[2,128,128]{2,1,0:T(8,128)}, f32[2,128,128]{2,1,0:T(8,128)S(1)}, u32[]{:S(2)}, u32[]{:S(2)}) %collective-permute-start.1) | collective-permute-done | bytes 131104 | tf_op jit(solution)/shard_map/while/body/eval_jaxpr/ppermute | solution.py:13
  382.7 7.4 %collective-permute-done.1 = f32[2,128,128]{2,1,0:T(8,128)S(1)} collective-permute-done((f32[2,128,128]{2,1,0:T(8,128)}, f32[2,128,128]{2,1,0:T(8,128)S(1)}, u32[]{:S(2)}, u32[]{:S(2)}) %collective-permute-start.1) | collective-permute-done | bytes 131104 | tf_op jit(solution)/shard_map/while/body/eval_jaxpr/ppermute | solution.py:13
  393.4 6.6 %collective-permute-done.1 = f32[2,128,128]{2,1,0:T(8,128)S(1)} collective-permute-done((f32[2,128,128]{2,1,0:T(8,128)}, f32[2,128,128]{2,1,0:T(8,128)S(1)}, u32[]{:S(2)}, u32[]{:S(2)}) %collective-permute-start.1) | collective-permute-done | bytes 131104 | tf_op jit(solution)/shard_map/while/body/eval_jaxpr/ppermute | solution.py:13
  403.3 6.4 %collective-permute-done.1 = f32[2,128,128]{2,1,0:T(8,128)S(1)} collective-permute-done((f32[2,128,128]{2,1,0:T(8,128)}, f32[2,128,128]{2,1,0:T(8,128)S(1)}, u32[]{:S(2)}, u32[]{:S(2)}) %collective-permute-start.1) | collective-permute-done | bytes 131104 | tf_op jit(solution)/shard_map/while/body/eval_jaxpr/ppermute | solution.py:13
  413.0 6.4 %collective-permute-done.1 = f32[2,128,128]{2,1,0:T(8,128)S(1)} collective-permute-done((f32[2,128,128]{2,1,0:T(8,128)}, f32[2,128,128]{2,1,0:T(8,128)S(1)}, u32[]{:S(2)}, u32[]{:S(2)}) %collective-permute-start.1) | collective-permute-done | bytes 131104 | tf_op jit(solution)/shard_map/while/body/eval_jaxpr/ppermute | solution.py:13
  422.7 6.4 %collective-permute-done.1 = f32[2,128,128]{2,1,0:T(8,128)S(1)} collective-permute-done((f32[2,128,128]{2,1,0:T(8,128)}, f32[2,128,128]{2,1,0:T(8,128)S(1)}, u32[]{:S(2)}, u32[]{:S(2)}) %collective-permute-start.1) | collective-permute-done | bytes 131104 | tf_op jit(solution)/shard_map/while/body/eval_jaxpr/ppermute | solution.py:13
  432.4 6.4 %collective-permute-done.1 = f32[2,128,128]{2,1,0:T(8,128)S(1)} collective-permute-done((f32[2,128,128]{2,1,0:T(8,128)}, f32[2,128,128]{2,1,0:T(8,128)S(1)}, u32[]{:S(2)}, u32[]{:S(2)}) %collective-permute-start.1) | collective-permute-done | bytes 131104 | tf_op jit(solution)/shard_map/while/body/eval_jaxpr/ppermute | solution.py:13
  442.1 6.4 %collective-permute-done.1 = f32[2,128,128]{2,1,0:T(8,128)S(1)} collective-permute-done((f32[2,128,128]{2,1,0:T(8,128)}, f32[2,128,128]{2,1,0:T(8,128)S(1)}, u32[]{:S(2)}, u32[]{:S(2)}) %collective-permute-start.1) | collective-permute-done | bytes 131104 | tf_op jit(solution)/shard_map/while/body/eval_jaxpr/ppermute | solution.py:13
  451.7 6.4 %collective-permute-done.1 = f32[2,128,128]{2,1,0:T(8,128)S(1)} collective-permute-done((f32[2,128,128]{2,1,0:T(8,128)}, f32[2,128,128]{2,1,0:T(8,128)S(1)}, u32[]{:S(2)}, u32[]{:S(2)}) %collective-permute-start.1) | collective-permute-done | bytes 131104 | tf_op jit(solution)/shard_map/while/body/eval_jaxpr/ppermute | solution.py:13
  (170 shorter events, 191.6 us)
Async XLA Ops:
  17.8 8.1 %collective-permute-start = (f32[2,128,128]{2,1,0:T(8,128)S(1)}, f32[2,128,128]{2,1,0:T(8,128)S(1)}, u32[]{:S(2)}, u32[]{:S(2)}) collective-permute-start(f32[2,128,128]{2,1,0:T(8,128)S(1)} %multiply_add_fusion.10), channel_id=1, source_target_pairs={{0,32},{32,64},{64,96},{96,128},{128,160},{160,192},{192,224},{224... | collective-permute-start | bytes 393224 | tf_op jit(solution)/shard_map/while/body/eval_jaxpr/ppermute | solution.py:13
  42.3 8.1 %collective-permute-start = (f32[2,128,128]{2,1,0:T(8,128)S(1)}, f32[2,128,128]{2,1,0:T(8,128)S(1)}, u32[]{:S(2)}, u32[]{:S(2)}) collective-permute-start(f32[2,128,128]{2,1,0:T(8,128)S(1)} %multiply_add_fusion.10), channel_id=1, source_target_pairs={{0,32},{32,64},{64,96},{96,128},{128,160},{160,192},{192,224},{224... | collective-permute-start | bytes 393224 | tf_op jit(solution)/shard_map/while/body/eval_jaxpr/ppermute | solution.py:13
  50.5 9.0 %collective-permute-start = (f32[2,128,128]{2,1,0:T(8,128)S(1)}, f32[2,128,128]{2,1,0:T(8,128)S(1)}, u32[]{:S(2)}, u32[]{:S(2)}) collective-permute-start(f32[2,128,128]{2,1,0:T(8,128)S(1)} %multiply_add_fusion.10), channel_id=1, source_target_pairs={{0,32},{32,64},{64,96},{96,128},{128,160},{160,192},{192,224},{224... | collective-permute-start | bytes 393224 | tf_op jit(solution)/shard_map/while/body/eval_jaxpr/ppermute | solution.py:13
  59.6 8.7 %collective-permute-start = (f32[2,128,128]{2,1,0:T(8,128)S(1)}, f32[2,128,128]{2,1,0:T(8,128)S(1)}, u32[]{:S(2)}, u32[]{:S(2)}) collective-permute-start(f32[2,128,128]{2,1,0:T(8,128)S(1)} %multiply_add_fusion.10), channel_id=1, source_target_pairs={{0,32},{32,64},{64,96},{96,128},{128,160},{160,192},{192,224},{224... | collective-permute-start | bytes 393224 | tf_op jit(solution)/shard_map/while/body/eval_jaxpr/ppermute | solution.py:13
  68.4 8.1 %collective-permute-start = (f32[2,128,128]{2,1,0:T(8,128)S(1)}, f32[2,128,128]{2,1,0:T(8,128)S(1)}, u32[]{:S(2)}, u32[]{:S(2)}) collective-permute-start(f32[2,128,128]{2,1,0:T(8,128)S(1)} %multiply_add_fusion.10), channel_id=1, source_target_pairs={{0,32},{32,64},{64,96},{96,128},{128,160},{160,192},{192,224},{224... | collective-permute-start | bytes 393224 | tf_op jit(solution)/shard_map/while/body/eval_jaxpr/ppermute | solution.py:13
  92.9 8.1 %collective-permute-start = (f32[2,128,128]{2,1,0:T(8,128)S(1)}, f32[2,128,128]{2,1,0:T(8,128)S(1)}, u32[]{:S(2)}, u32[]{:S(2)}) collective-permute-start(f32[2,128,128]{2,1,0:T(8,128)S(1)} %multiply_add_fusion.10), channel_id=1, source_target_pairs={{0,32},{32,64},{64,96},{96,128},{128,160},{160,192},{192,224},{224... | collective-permute-start | bytes 393224 | tf_op jit(solution)/shard_map/while/body/eval_jaxpr/ppermute | solution.py:13
  101.1 8.6 %collective-permute-start = (f32[2,128,128]{2,1,0:T(8,128)S(1)}, f32[2,128,128]{2,1,0:T(8,128)S(1)}, u32[]{:S(2)}, u32[]{:S(2)}) collective-permute-start(f32[2,128,128]{2,1,0:T(8,128)S(1)} %multiply_add_fusion.10), channel_id=1, source_target_pairs={{0,32},{32,64},{64,96},{96,128},{128,160},{160,192},{192,224},{224... | collective-permute-start | bytes 393224 | tf_op jit(solution)/shard_map/while/body/eval_jaxpr/ppermute | solution.py:13
  109.8 9.2 %collective-permute-start = (f32[2,128,128]{2,1,0:T(8,128)S(1)}, f32[2,128,128]{2,1,0:T(8,128)S(1)}, u32[]{:S(2)}, u32[]{:S(2)}) collective-permute-start(f32[2,128,128]{2,1,0:T(8,128)S(1)} %multiply_add_fusion.10), channel_id=1, source_target_pairs={{0,32},{32,64},{64,96},{96,128},{128,160},{160,192},{192,224},{224... | collective-permute-start | bytes 393224 | tf_op jit(solution)/shard_map/while/body/eval_jaxpr/ppermute | solution.py:13
  119.0 8.1 %collective-permute-start = (f32[2,128,128]{2,1,0:T(8,128)S(1)}, f32[2,128,128]{2,1,0:T(8,128)S(1)}, u32[]{:S(2)}, u32[]{:S(2)}) collective-permute-start(f32[2,128,128]{2,1,0:T(8,128)S(1)} %multiply_add_fusion.10), channel_id=1, source_target_pairs={{0,32},{32,64},{64,96},{96,128},{128,160},{160,192},{192,224},{224... | collective-permute-start | bytes 393224 | tf_op jit(solution)/shard_map/while/body/eval_jaxpr/ppermute | solution.py:13
  312.1 8.6 %collective-permute-start.1 = (f32[2,128,128]{2,1,0:T(8,128)}, f32[2,128,128]{2,1,0:T(8,128)S(1)}, u32[]{:S(2)}, u32[]{:S(2)}) collective-permute-start(f32[2,128,128]{2,1,0:T(8,128)} %multiply_add_fusion.11), channel_id=1, source_target_pairs={{32,0},{64,32},{96,64},{128,96},{160,128},{192,160},{224,192},{256... | collective-permute-start | bytes 393224 | tf_op jit(solution)/shard_map/while/body/eval_jaxpr/ppermute | solution.py:13
  322.1 8.3 %collective-permute-start.1 = (f32[2,128,128]{2,1,0:T(8,128)}, f32[2,128,128]{2,1,0:T(8,128)S(1)}, u32[]{:S(2)}, u32[]{:S(2)}) collective-permute-start(f32[2,128,128]{2,1,0:T(8,128)} %multiply_add_fusion.11), channel_id=1, source_target_pairs={{32,0},{64,32},{96,64},{128,96},{160,128},{192,160},{224,192},{256... | collective-permute-start | bytes 393224 | tf_op jit(solution)/shard_map/while/body/eval_jaxpr/ppermute | solution.py:13
  331.8 8.3 %collective-permute-start.1 = (f32[2,128,128]{2,1,0:T(8,128)}, f32[2,128,128]{2,1,0:T(8,128)S(1)}, u32[]{:S(2)}, u32[]{:S(2)}) collective-permute-start(f32[2,128,128]{2,1,0:T(8,128)} %multiply_add_fusion.11), channel_id=1, source_target_pairs={{32,0},{64,32},{96,64},{128,96},{160,128},{192,160},{224,192},{256... | collective-permute-start | bytes 393224 | tf_op jit(solution)/shard_map/while/body/eval_jaxpr/ppermute | solution.py:13
  341.5 8.3 %collective-permute-start.1 = (f32[2,128,128]{2,1,0:T(8,128)}, f32[2,128,128]{2,1,0:T(8,128)S(1)}, u32[]{:S(2)}, u32[]{:S(2)}) collective-permute-start(f32[2,128,128]{2,1,0:T(8,128)} %multiply_add_fusion.11), channel_id=1, source_target_pairs={{32,0},{64,32},{96,64},{128,96},{160,128},{192,160},{224,192},{256... | collective-permute-start | bytes 393224 | tf_op jit(solution)/shard_map/while/body/eval_jaxpr/ppermute | solution.py:13
  351.2 8.3 %collective-permute-start.1 = (f32[2,128,128]{2,1,0:T(8,128)}, f32[2,128,128]{2,1,0:T(8,128)S(1)}, u32[]{:S(2)}, u32[]{:S(2)}) collective-permute-start(f32[2,128,128]{2,1,0:T(8,128)} %multiply_add_fusion.11), channel_id=1, source_target_pairs={{32,0},{64,32},{96,64},{128,96},{160,128},{192,160},{224,192},{256... | collective-permute-start | bytes 393224 | tf_op jit(solution)/shard_map/while/body/eval_jaxpr/ppermute | solution.py:13
  360.8 8.3 %collective-permute-start.1 = (f32[2,128,128]{2,1,0:T(8,128)}, f32[2,128,128]{2,1,0:T(8,128)S(1)}, u32[]{:S(2)}, u32[]{:S(2)}) collective-permute-start(f32[2,128,128]{2,1,0:T(8,128)} %multiply_add_fusion.11), channel_id=1, source_target_pairs={{32,0},{64,32},{96,64},{128,96},{160,128},{192,160},{224,192},{256... | collective-permute-start | bytes 393224 | tf_op jit(solution)/shard_map/while/body/eval_jaxpr/ppermute | solution.py:13
  370.5 8.9 %collective-permute-start.1 = (f32[2,128,128]{2,1,0:T(8,128)}, f32[2,128,128]{2,1,0:T(8,128)S(1)}, u32[]{:S(2)}, u32[]{:S(2)}) collective-permute-start(f32[2,128,128]{2,1,0:T(8,128)} %multiply_add_fusion.11), channel_id=1, source_target_pairs={{32,0},{64,32},{96,64},{128,96},{160,128},{192,160},{224,192},{256... | collective-permute-start | bytes 393224 | tf_op jit(solution)/shard_map/while/body/eval_jaxpr/ppermute | solution.py:13
  380.8 9.3 %collective-permute-start.1 = (f32[2,128,128]{2,1,0:T(8,128)}, f32[2,128,128]{2,1,0:T(8,128)S(1)}, u32[]{:S(2)}, u32[]{:S(2)}) collective-permute-start(f32[2,128,128]{2,1,0:T(8,128)} %multiply_add_fusion.11), channel_id=1, source_target_pairs={{32,0},{64,32},{96,64},{128,96},{160,128},{192,160},{224,192},{256... | collective-permute-start | bytes 393224 | tf_op jit(solution)/shard_map/while/body/eval_jaxpr/ppermute | solution.py:13
  391.5 8.5 %collective-permute-start.1 = (f32[2,128,128]{2,1,0:T(8,128)}, f32[2,128,128]{2,1,0:T(8,128)S(1)}, u32[]{:S(2)}, u32[]{:S(2)}) collective-permute-start(f32[2,128,128]{2,1,0:T(8,128)} %multiply_add_fusion.11), channel_id=1, source_target_pairs={{32,0},{64,32},{96,64},{128,96},{160,128},{192,160},{224,192},{256... | collective-permute-start | bytes 393224 | tf_op jit(solution)/shard_map/while/body/eval_jaxpr/ppermute | solution.py:13
  401.4 8.3 %collective-permute-start.1 = (f32[2,128,128]{2,1,0:T(8,128)}, f32[2,128,128]{2,1,0:T(8,128)S(1)}, u32[]{:S(2)}, u32[]{:S(2)}) collective-permute-start(f32[2,128,128]{2,1,0:T(8,128)} %multiply_add_fusion.11), channel_id=1, source_target_pairs={{32,0},{64,32},{96,64},{128,96},{160,128},{192,160},{224,192},{256... | collective-permute-start | bytes 393224 | tf_op jit(solution)/shard_map/while/body/eval_jaxpr/ppermute | solution.py:13
  411.1 8.3 %collective-permute-start.1 = (f32[2,128,128]{2,1,0:T(8,128)}, f32[2,128,128]{2,1,0:T(8,128)S(1)}, u32[]{:S(2)}, u32[]{:S(2)}) collective-permute-start(f32[2,128,128]{2,1,0:T(8,128)} %multiply_add_fusion.11), channel_id=1, source_target_pairs={{32,0},{64,32},{96,64},{128,96},{160,128},{192,160},{224,192},{256... | collective-permute-start | bytes 393224 | tf_op jit(solution)/shard_map/while/body/eval_jaxpr/ppermute | solution.py:13
  420.8 8.3 %collective-permute-start.1 = (f32[2,128,128]{2,1,0:T(8,128)}, f32[2,128,128]{2,1,0:T(8,128)S(1)}, u32[]{:S(2)}, u32[]{:S(2)}) collective-permute-start(f32[2,128,128]{2,1,0:T(8,128)} %multiply_add_fusion.11), channel_id=1, source_target_pairs={{32,0},{64,32},{96,64},{128,96},{160,128},{192,160},{224,192},{256... | collective-permute-start | bytes 393224 | tf_op jit(solution)/shard_map/while/body/eval_jaxpr/ppermute | solution.py:13
  430.5 8.3 %collective-permute-start.1 = (f32[2,128,128]{2,1,0:T(8,128)}, f32[2,128,128]{2,1,0:T(8,128)S(1)}, u32[]{:S(2)}, u32[]{:S(2)}) collective-permute-start(f32[2,128,128]{2,1,0:T(8,128)} %multiply_add_fusion.11), channel_id=1, source_target_pairs={{32,0},{64,32},{96,64},{128,96},{160,128},{192,160},{224,192},{256... | collective-permute-start | bytes 393224 | tf_op jit(solution)/shard_map/while/body/eval_jaxpr/ppermute | solution.py:13
  440.1 8.3 %collective-permute-start.1 = (f32[2,128,128]{2,1,0:T(8,128)}, f32[2,128,128]{2,1,0:T(8,128)S(1)}, u32[]{:S(2)}, u32[]{:S(2)}) collective-permute-start(f32[2,128,128]{2,1,0:T(8,128)} %multiply_add_fusion.11), channel_id=1, source_target_pairs={{32,0},{64,32},{96,64},{128,96},{160,128},{192,160},{224,192},{256... | collective-permute-start | bytes 393224 | tf_op jit(solution)/shard_map/while/body/eval_jaxpr/ppermute | solution.py:13
  449.8 8.3 %collective-permute-start.1 = (f32[2,128,128]{2,1,0:T(8,128)}, f32[2,128,128]{2,1,0:T(8,128)S(1)}, u32[]{:S(2)}, u32[]{:S(2)}) collective-permute-start(f32[2,128,128]{2,1,0:T(8,128)} %multiply_add_fusion.11), channel_id=1, source_target_pairs={{32,0},{64,32},{96,64},{128,96},{160,128},{192,160},{224,192},{256... | collective-permute-start | bytes 393224 | tf_op jit(solution)/shard_map/while/body/eval_jaxpr/ppermute | solution.py:13
  (30 other events, 869.6 us)
where the time goes:
time: 473 us; the launch traced here: 471 us
  blocking collectives  158 us (33%)
  waiting for transfers between devices  138 us (29%)
  starting transfers between devices  112 us (24%)
  other arithmetic  29.4 us (6%)
  matrix products  20.7 us (4%)
  local copies, waits for them, and re-layouts  11.8 us (2%)
    ppermute x30, waiting for transfers between devices, passed_along(): lax.ppermute(value, axis, [(source, source + steps) for source in range(i...  138 us
    ppermute x30, starting transfers between devices, passed_along(): lax.ppermute(value, axis, [(source, source + steps) for source in range(i...  112 us
    psum x1, blocking collectives, local(): squares = lax.psum(jnp.sum(flattened * flattened, axis=1), 'head')  62.7 us
    psum x1, blocking collectives, local(): projected = lax.psum(jnp.sum(normed_grad * normed, axis=1), 'head')  62.7 us
    psum x1, blocking collectives, local(): gain_grad = lax.psum(gain_part, 'seq')  32.4 us
    add x15, other arithmetic, relay_step(): outgoing = jnp.exp(device_decay)[:, None, None] * suffix + device_back  21.1 us
  transfers between devices with their start and end apart: 30, of which 30 were waited for; matrix products, arithmetic and copies ran while one was open for 0% of the time, Pallas kernels for 0%

commit v1 on v0

--- a/solution.py
+++ b/solution.py
@@ -1,3 +1,4 @@
+import functools
 import jax
 import jax.numpy as jnp
 from jax import lax
@@ -5,6 +6,13 @@
 
 epsilon = 1e-06
 highest = lax.Precision.HIGHEST
+
+
+def expand_sides(arr, axis_name):
+    return jnp.sum(lax.all_gather(arr, axis_name), axis=0)
+
+
+number_view = functools.partial(expand_sides, axis_name="head")
 
 
 def passed_along(value, axis, steps):
@@ -92,7 +100,7 @@
     squares = lax.psum(jnp.sum(flattened * flattened, axis=1), "head")
     inverse = 1.0 / jnp.sqrt(squares / total_channels + epsilon)
     normed = flattened * inverse[:, None]
-    projected = lax.psum(jnp.sum(normed_grad * normed, axis=1), "head")
+    projected = number_view(jnp.sum(normed_grad * normed, axis=1))
     output = (normed * gain).astype(jnp.bfloat16)
     gain_part = jnp.sum(grad_wide * normed, axis=0)
     flat_grad = (normed_grad - normed * (projected / total_channels)[:, None]) * inverse[:, None]

time: 473 us -> 434 us (0.918)
  the two profiles are of different devices: /device:TPU:96 before, /device:TPU:98 now
where the time goes in v1:
time: 434 us; the launch traced here: 433 us
  waiting for transfers between devices  139 us (32%)
  blocking collectives  117 us (27%)
  starting transfers between devices  112 us (26%)
  other arithmetic  30.2 us (7%)
  matrix products  20.7 us (5%)
  local copies, waits for them, and re-layouts  11.9 us (3%)
    ppermute x30, waiting for transfers between devices, passed_along(): lax.ppermute(value, axis, [(source, source + steps) for source in range(i...  139 us
    ppermute x30, starting transfers between devices, passed_along(): lax.ppermute(value, axis, [(source, source + steps) for source in range(i...  112 us
    psum x1, blocking collectives, local(): squares = lax.psum(jnp.sum(flattened * flattened, axis=1), 'head')  53 us
    psum x1, blocking collectives, local(): gain_grad = lax.psum(gain_part, 'seq')  32.4 us
    all_gather x1, blocking collectives, expand_sides(): return jnp.sum(lax.all_gather(arr, axis_name), axis=0)  32 us
    add x15, other arithmetic, relay_step(): outgoing = jnp.exp(device_decay)[:, None, None] * suffix + device_back  21.2 us
  transfers between devices with their start and end apart: 30, of which 30 were waited for; matrix products, arithmetic and copies ran while one was open for 0% of the time, Pallas kernels for 0%

profile of v1, /device:TPU:98, one launch (start us, length us, event | category | flops | bytes accessed | tf_op | source)
XLA Modules:
  0.0 432.5 jit_solution(11748013301325978053)
XLA Ops:
  9.9 125.4 %while.24 = (s32[]{:T(128)}, f32[2,128,128]{2,1,0:T(8,128)S(1)}, f32[2,1,1]{0,2,1:T(1,128)S(1)}, f32[2,128,128]{2,1,0:T(8,128)S(1)}, s32[]{:T(128)}) while((s32[]{:T(128)}, f32[2,128,128]{2,1,0:T(8,128)S(1)}, f32[2,1,1]{0,2,1:T(1,128)S(1)}, f32[2,128,128]{2,1,0:T(8,128)S(1)}, s32[]{:T(128)}) %tuple.63), condition=%wide.region_4.5_spmd, body=%wide.region_3.4_spmd.sunk | while | flops 65538 | bytes 917613 | solution.py:40
  59.6 5.6 %collective-permute-start = (f32[2,128,128]{2,1,0:T(8,128)S(1)}, f32[2,128,128]{2,1,0:T(8,128)S(1)}, u32[]{:S(2)}, u32[]{:S(2)}) collective-permute-start(f32[2,128,128]{2,1,0:T(8,128)S(1)} %multiply_add_fusion.10), channel_id=1, source_target_pairs={{0,32},{32,64},{64,96},{96,128},{128,160},{160,192},{192,224},{224... | collective-permute-start | bytes 393224 | tf_op jit(solution)/shard_map/while/body/eval_jaxpr/ppermute | solution.py:21
  68.4 5.6 %collective-permute-start = (f32[2,128,128]{2,1,0:T(8,128)S(1)}, f32[2,128,128]{2,1,0:T(8,128)S(1)}, u32[]{:S(2)}, u32[]{:S(2)}) collective-permute-start(f32[2,128,128]{2,1,0:T(8,128)S(1)} %multiply_add_fusion.10), channel_id=1, source_target_pairs={{0,32},{32,64},{64,96},{96,128},{128,160},{160,192},{192,224},{224... | collective-permute-start | bytes 393224 | tf_op jit(solution)/shard_map/while/body/eval_jaxpr/ppermute | solution.py:21
  119.0 5.6 %collective-permute-start = (f32[2,128,128]{2,1,0:T(8,128)S(1)}, f32[2,128,128]{2,1,0:T(8,128)S(1)}, u32[]{:S(2)}, u32[]{:S(2)}) collective-permute-start(f32[2,128,128]{2,1,0:T(8,128)S(1)} %multiply_add_fusion.10), channel_id=1, source_target_pairs={{0,32},{32,64},{64,96},{96,128},{128,160},{160,192},{192,224},{224... | collective-permute-start | bytes 393224 | tf_op jit(solution)/shard_map/while/body/eval_jaxpr/ppermute | solution.py:21
  139.9 53.0 %psum.14 = f32[1024]{0:T(1024)S(1)} all-reduce(f32[1024]{0:T(1024)S(1)} %bitcast.231), channel_id=1, replica_groups=mesh['seq'=16,'head'=32] {'head'}, use_global_device_ids=true, to_apply=%region_6.7 | all-reduce | flops 1024 | bytes 8192 | tf_op jit(solution)/shard_map/psum | solution.py:100
  195.1 32.4 %psum.15 = f32[256]{0:T(256)} all-reduce(f32[256]{0:T(256)S(1)} %get-tuple-element.107), channel_id=1, replica_groups=mesh['seq'=16,'head'=32] {'seq'}, use_global_device_ids=true, to_apply=%region_12.13 | all-reduce | flops 256 | bytes 2048 | tf_op jit(solution)/shard_map/psum | solution.py:141
  227.5 32.0 %all-gather = f32[32768]{0:T(1024)S(1)} all-gather(f32[1024]{0:T(1024)S(1)} %get-tuple-element.108), channel_id=2, replica_groups=mesh['seq'=16,'head'=32] {'head'}, dimensions={0}, use_global_device_ids=true | all-gather | bytes 135168 | tf_op jit(solution)/shard_map/all_gather | solution.py:12
  263.5 6.1 %convolution_bitcast_fusion.4 = f32[4,256,2,128]{3,1,0,2:T(8,128)} fusion(f32[2,4,256,256]{3,2,1,0:T(8,128)} %copy-done, f32[4,256,2,128]{3,2,1,0:T(2,128)S(1)} %reshape.131), kind=kOutput, calls=%fused_computation.11 | convolution fusion | flops 805306368 | bytes 4194304 | tf_op jit(solution)/shard_map/hnij,hnid->hnjd/dot_general | solution.py:116
  271.0 148.2 %while.25 = (s32[]{:T(128)}, f32[2,128,128]{2,1,0:T(8,128)S(1)}, f32[2,1,1]{0,2,1:T(1,128)}, f32[2,128,128]{2,1,0:T(8,128)S(1)}, s32[]{:T(128)}) while((s32[]{:T(128)}, f32[2,128,128]{2,1,0:T(8,128)S(1)}, f32[2,1,1]{0,2,1:T(1,128)}, f32[2,128,128]{2,1,0:T(8,128)S(1)}, s32[]{:T(128)}) %tuple.69), condition=%wide.region_10.11_spmd, body=%wide.region_9.10_spmd.sunk | while | flops 65538 | bytes 917613 | solution.py:49
  274.5 7.1 %collective-permute-done.1 = f32[2,128,128]{2,1,0:T(8,128)S(1)} collective-permute-done((f32[2,128,128]{2,1,0:T(8,128)}, f32[2,128,128]{2,1,0:T(8,128)S(1)}, u32[]{:S(2)}, u32[]{:S(2)}) %collective-permute-start.1) | collective-permute-done | bytes 131104 | tf_op jit(solution)/shard_map/while/body/eval_jaxpr/ppermute | solution.py:21
  285.0 6.4 %collective-permute-done.1 = f32[2,128,128]{2,1,0:T(8,128)S(1)} collective-permute-done((f32[2,128,128]{2,1,0:T(8,128)}, f32[2,128,128]{2,1,0:T(8,128)S(1)}, u32[]{:S(2)}, u32[]{:S(2)}) %collective-permute-start.1) | collective-permute-done | bytes 131104 | tf_op jit(solution)/shard_map/while/body/eval_jaxpr/ppermute | solution.py:21
  294.7 6.4 %collective-permute-done.1 = f32[2,128,128]{2,1,0:T(8,128)S(1)} collective-permute-done((f32[2,128,128]{2,1,0:T(8,128)}, f32[2,128,128]{2,1,0:T(8,128)S(1)}, u32[]{:S(2)}, u32[]{:S(2)}) %collective-permute-start.1) | collective-permute-done | bytes 131104 | tf_op jit(solution)/shard_map/while/body/eval_jaxpr/ppermute | solution.py:21
  304.4 6.4 %collective-permute-done.1 = f32[2,128,128]{2,1,0:T(8,128)S(1)} collective-permute-done((f32[2,128,128]{2,1,0:T(8,128)}, f32[2,128,128]{2,1,0:T(8,128)S(1)}, u32[]{:S(2)}, u32[]{:S(2)}) %collective-permute-start.1) | collective-permute-done | bytes 131104 | tf_op jit(solution)/shard_map/while/body/eval_jaxpr/ppermute | solution.py:21
  314.1 6.4 %collective-permute-done.1 = f32[2,128,128]{2,1,0:T(8,128)S(1)} collective-permute-done((f32[2,128,128]{2,1,0:T(8,128)}, f32[2,128,128]{2,1,0:T(8,128)S(1)}, u32[]{:S(2)}, u32[]{:S(2)}) %collective-permute-start.1) | collective-permute-done | bytes 131104 | tf_op jit(solution)/shard_map/while/body/eval_jaxpr/ppermute | solution.py:21
  323.8 6.4 %collective-permute-done.1 = f32[2,128,128]{2,1,0:T(8,128)S(1)} collective-permute-done((f32[2,128,128]{2,1,0:T(8,128)}, f32[2,128,128]{2,1,0:T(8,128)S(1)}, u32[]{:S(2)}, u32[]{:S(2)}) %collective-permute-start.1) | collective-permute-done | bytes 131104 | tf_op jit(solution)/shard_map/while/body/eval_jaxpr/ppermute | solution.py:21
  333.4 6.4 %collective-permute-done.1 = f32[2,128,128]{2,1,0:T(8,128)S(1)} collective-permute-done((f32[2,128,128]{2,1,0:T(8,128)}, f32[2,128,128]{2,1,0:T(8,128)S(1)}, u32[]{:S(2)}, u32[]{:S(2)}) %collective-permute-start.1) | collective-permute-done | bytes 131104 | tf_op jit(solution)/shard_map/while/body/eval_jaxpr/ppermute | solution.py:21
  343.2 7.6 %collective-permute-done.1 = f32[2,128,128]{2,1,0:T(8,128)S(1)} collective-permute-done((f32[2,128,128]{2,1,0:T(8,128)}, f32[2,128,128]{2,1,0:T(8,128)S(1)}, u32[]{:S(2)}, u32[]{:S(2)}) %collective-permute-start.1) | collective-permute-done | bytes 131104 | tf_op jit(solution)/shard_map/while/body/eval_jaxpr/ppermute | solution.py:21
  354.2 6.9 %collective-permute-done.1 = f32[2,128,128]{2,1,0:T(8,128)S(1)} collective-permute-done((f32[2,128,128]{2,1,0:T(8,128)}, f32[2,128,128]{2,1,0:T(8,128)S(1)}, u32[]{:S(2)}, u32[]{:S(2)}) %collective-permute-start.1) | collective-permute-done | bytes 131104 | tf_op jit(solution)/shard_map/while/body/eval_jaxpr/ppermute | solution.py:21
  364.4 6.4 %collective-permute-done.1 = f32[2,128,128]{2,1,0:T(8,128)S(1)} collective-permute-done((f32[2,128,128]{2,1,0:T(8,128)}, f32[2,128,128]{2,1,0:T(8,128)S(1)}, u32[]{:S(2)}, u32[]{:S(2)}) %collective-permute-start.1) | collective-permute-done | bytes 131104 | tf_op jit(solution)/shard_map/while/body/eval_jaxpr/ppermute | solution.py:21
  374.1 6.4 %collective-permute-done.1 = f32[2,128,128]{2,1,0:T(8,128)S(1)} collective-permute-done((f32[2,128,128]{2,1,0:T(8,128)}, f32[2,128,128]{2,1,0:T(8,128)S(1)}, u32[]{:S(2)}, u32[]{:S(2)}) %collective-permute-start.1) | collective-permute-done | bytes 131104 | tf_op jit(solution)/shard_map/while/body/eval_jaxpr/ppermute | solution.py:21
  383.8 6.4 %collective-permute-done.1 = f32[2,128,128]{2,1,0:T(8,128)S(1)} collective-permute-done((f32[2,128,128]{2,1,0:T(8,128)}, f32[2,128,128]{2,1,0:T(8,128)S(1)}, u32[]{:S(2)}, u32[]{:S(2)}) %collective-permute-start.1) | collective-permute-done | bytes 131104 | tf_op jit(solution)/shard_map/while/body/eval_jaxpr/ppermute | solution.py:21
  393.5 6.4 %collective-permute-done.1 = f32[2,128,128]{2,1,0:T(8,128)S(1)} collective-permute-done((f32[2,128,128]{2,1,0:T(8,128)}, f32[2,128,128]{2,1,0:T(8,128)S(1)}, u32[]{:S(2)}, u32[]{:S(2)}) %collective-permute-start.1) | collective-permute-done | bytes 131104 | tf_op jit(solution)/shard_map/while/body/eval_jaxpr/ppermute | solution.py:21
  403.1 6.4 %collective-permute-done.1 = f32[2,128,128]{2,1,0:T(8,128)S(1)} collective-permute-done((f32[2,128,128]{2,1,0:T(8,128)}, f32[2,128,128]{2,1,0:T(8,128)S(1)}, u32[]{:S(2)}, u32[]{:S(2)}) %collective-permute-start.1) | collective-permute-done | bytes 131104 | tf_op jit(solution)/shard_map/while/body/eval_jaxpr/ppermute | solution.py:21
  412.8 6.4 %collective-permute-done.1 = f32[2,128,128]{2,1,0:T(8,128)S(1)} collective-permute-done((f32[2,128,128]{2,1,0:T(8,128)}, f32[2,128,128]{2,1,0:T(8,128)S(1)}, u32[]{:S(2)}, u32[]{:S(2)}) %collective-permute-start.1) | collective-permute-done | bytes 131104 | tf_op jit(solution)/shard_map/while/body/eval_jaxpr/ppermute | solution.py:21
  (174 shorter events, 192.5 us)
Async XLA Ops:
  17.8 8.1 %collective-permute-start = (f32[2,128,128]{2,1,0:T(8,128)S(1)}, f32[2,128,128]{2,1,0:T(8,128)S(1)}, u32[]{:S(2)}, u32[]{:S(2)}) collective-permute-start(f32[2,128,128]{2,1,0:T(8,128)S(1)} %multiply_add_fusion.10), channel_id=1, source_target_pairs={{0,32},{32,64},{64,96},{96,128},{128,160},{160,192},{192,224},{224... | collective-permute-start | bytes 393224 | tf_op jit(solution)/shard_map/while/body/eval_jaxpr/ppermute | solution.py:21
  26.0 8.1 %collective-permute-start = (f32[2,128,128]{2,1,0:T(8,128)S(1)}, f32[2,128,128]{2,1,0:T(8,128)S(1)}, u32[]{:S(2)}, u32[]{:S(2)}) collective-permute-start(f32[2,128,128]{2,1,0:T(8,128)S(1)} %multiply_add_fusion.10), channel_id=1, source_target_pairs={{0,32},{32,64},{64,96},{96,128},{128,160},{160,192},{192,224},{224... | collective-permute-start | bytes 393224 | tf_op jit(solution)/shard_map/while/body/eval_jaxpr/ppermute | solution.py:21
  50.5 9.0 %collective-permute-start = (f32[2,128,128]{2,1,0:T(8,128)S(1)}, f32[2,128,128]{2,1,0:T(8,128)S(1)}, u32[]{:S(2)}, u32[]{:S(2)}) collective-permute-start(f32[2,128,128]{2,1,0:T(8,128)S(1)} %multiply_add_fusion.10), channel_id=1, source_target_pairs={{0,32},{32,64},{64,96},{96,128},{128,160},{160,192},{192,224},{224... | collective-permute-start | bytes 393224 | tf_op jit(solution)/shard_map/while/body/eval_jaxpr/ppermute | solution.py:21
  59.6 8.7 %collective-permute-start = (f32[2,128,128]{2,1,0:T(8,128)S(1)}, f32[2,128,128]{2,1,0:T(8,128)S(1)}, u32[]{:S(2)}, u32[]{:S(2)}) collective-permute-start(f32[2,128,128]{2,1,0:T(8,128)S(1)} %multiply_add_fusion.10), channel_id=1, source_target_pairs={{0,32},{32,64},{64,96},{96,128},{128,160},{160,192},{192,224},{224... | collective-permute-start | bytes 393224 | tf_op jit(solution)/shard_map/while/body/eval_jaxpr/ppermute | solution.py:21
  68.4 8.1 %collective-permute-start = (f32[2,128,128]{2,1,0:T(8,128)S(1)}, f32[2,128,128]{2,1,0:T(8,128)S(1)}, u32[]{:S(2)}, u32[]{:S(2)}) collective-permute-start(f32[2,128,128]{2,1,0:T(8,128)S(1)} %multiply_add_fusion.10), channel_id=1, source_target_pairs={{0,32},{32,64},{64,96},{96,128},{128,160},{160,192},{192,224},{224... | collective-permute-start | bytes 393224 | tf_op jit(solution)/shard_map/while/body/eval_jaxpr/ppermute | solution.py:21
  76.6 8.1 %collective-permute-start = (f32[2,128,128]{2,1,0:T(8,128)S(1)}, f32[2,128,128]{2,1,0:T(8,128)S(1)}, u32[]{:S(2)}, u32[]{:S(2)}) collective-permute-start(f32[2,128,128]{2,1,0:T(8,128)S(1)} %multiply_add_fusion.10), channel_id=1, source_target_pairs={{0,32},{32,64},{64,96},{96,128},{128,160},{160,192},{192,224},{224... | collective-permute-start | bytes 393224 | tf_op jit(solution)/shard_map/while/body/eval_jaxpr/ppermute | solution.py:21
  101.1 8.6 %collective-permute-start = (f32[2,128,128]{2,1,0:T(8,128)S(1)}, f32[2,128,128]{2,1,0:T(8,128)S(1)}, u32[]{:S(2)}, u32[]{:S(2)}) collective-permute-start(f32[2,128,128]{2,1,0:T(8,128)S(1)} %multiply_add_fusion.10), channel_id=1, source_target_pairs={{0,32},{32,64},{64,96},{96,128},{128,160},{160,192},{192,224},{224... | collective-permute-start | bytes 393224 | tf_op jit(solution)/shard_map/while/body/eval_jaxpr/ppermute | solution.py:21
  109.8 9.2 %collective-permute-start = (f32[2,128,128]{2,1,0:T(8,128)S(1)}, f32[2,128,128]{2,1,0:T(8,128)S(1)}, u32[]{:S(2)}, u32[]{:S(2)}) collective-permute-start(f32[2,128,128]{2,1,0:T(8,128)S(1)} %multiply_add_fusion.10), channel_id=1, source_target_pairs={{0,32},{32,64},{64,96},{96,128},{128,160},{160,192},{192,224},{224... | collective-permute-start | bytes 393224 | tf_op jit(solution)/shard_map/while/body/eval_jaxpr/ppermute | solution.py:21
  119.0 8.1 %collective-permute-start = (f32[2,128,128]{2,1,0:T(8,128)S(1)}, f32[2,128,128]{2,1,0:T(8,128)S(1)}, u32[]{:S(2)}, u32[]{:S(2)}) collective-permute-start(f32[2,128,128]{2,1,0:T(8,128)S(1)} %multiply_add_fusion.10), channel_id=1, source_target_pairs={{0,32},{32,64},{64,96},{96,128},{128,160},{160,192},{192,224},{224... | collective-permute-start | bytes 393224 | tf_op jit(solution)/shard_map/while/body/eval_jaxpr/ppermute | solution.py:21
  272.6 9.0 %collective-permute-start.1 = (f32[2,128,128]{2,1,0:T(8,128)}, f32[2,128,128]{2,1,0:T(8,128)S(1)}, u32[]{:S(2)}, u32[]{:S(2)}) collective-permute-start(f32[2,128,128]{2,1,0:T(8,128)} %multiply_add_fusion.11), channel_id=1, source_target_pairs={{32,0},{64,32},{96,64},{128,96},{160,128},{192,160},{224,192},{256... | collective-permute-start | bytes 393224 | tf_op jit(solution)/shard_map/while/body/eval_jaxpr/ppermute | solution.py:21
  283.1 8.3 %collective-permute-start.1 = (f32[2,128,128]{2,1,0:T(8,128)}, f32[2,128,128]{2,1,0:T(8,128)S(1)}, u32[]{:S(2)}, u32[]{:S(2)}) collective-permute-start(f32[2,128,128]{2,1,0:T(8,128)} %multiply_add_fusion.11), channel_id=1, source_target_pairs={{32,0},{64,32},{96,64},{128,96},{160,128},{192,160},{224,192},{256... | collective-permute-start | bytes 393224 | tf_op jit(solution)/shard_map/while/body/eval_jaxpr/ppermute | solution.py:21
  292.8 8.3 %collective-permute-start.1 = (f32[2,128,128]{2,1,0:T(8,128)}, f32[2,128,128]{2,1,0:T(8,128)S(1)}, u32[]{:S(2)}, u32[]{:S(2)}) collective-permute-start(f32[2,128,128]{2,1,0:T(8,128)} %multiply_add_fusion.11), channel_id=1, source_target_pairs={{32,0},{64,32},{96,64},{128,96},{160,128},{192,160},{224,192},{256... | collective-permute-start | bytes 393224 | tf_op jit(solution)/shard_map/while/body/eval_jaxpr/ppermute | solution.py:21
  302.5 8.3 %collective-permute-start.1 = (f32[2,128,128]{2,1,0:T(8,128)}, f32[2,128,128]{2,1,0:T(8,128)S(1)}, u32[]{:S(2)}, u32[]{:S(2)}) collective-permute-start(f32[2,128,128]{2,1,0:T(8,128)} %multiply_add_fusion.11), channel_id=1, source_target_pairs={{32,0},{64,32},{96,64},{128,96},{160,128},{192,160},{224,192},{256... | collective-permute-start | bytes 393224 | tf_op jit(solution)/shard_map/while/body/eval_jaxpr/ppermute | solution.py:21
  312.1 8.3 %collective-permute-start.1 = (f32[2,128,128]{2,1,0:T(8,128)}, f32[2,128,128]{2,1,0:T(8,128)S(1)}, u32[]{:S(2)}, u32[]{:S(2)}) collective-permute-start(f32[2,128,128]{2,1,0:T(8,128)} %multiply_add_fusion.11), channel_id=1, source_target_pairs={{32,0},{64,32},{96,64},{128,96},{160,128},{192,160},{224,192},{256... | collective-permute-start | bytes 393224 | tf_op jit(solution)/shard_map/while/body/eval_jaxpr/ppermute | solution.py:21
  321.8 8.3 %collective-permute-start.1 = (f32[2,128,128]{2,1,0:T(8,128)}, f32[2,128,128]{2,1,0:T(8,128)S(1)}, u32[]{:S(2)}, u32[]{:S(2)}) collective-permute-start(f32[2,128,128]{2,1,0:T(8,128)} %multiply_add_fusion.11), channel_id=1, source_target_pairs={{32,0},{64,32},{96,64},{128,96},{160,128},{192,160},{224,192},{256... | collective-permute-start | bytes 393224 | tf_op jit(solution)/shard_map/while/body/eval_jaxpr/ppermute | solution.py:21
  331.5 8.4 %collective-permute-start.1 = (f32[2,128,128]{2,1,0:T(8,128)}, f32[2,128,128]{2,1,0:T(8,128)S(1)}, u32[]{:S(2)}, u32[]{:S(2)}) collective-permute-start(f32[2,128,128]{2,1,0:T(8,128)} %multiply_add_fusion.11), channel_id=1, source_target_pairs={{32,0},{64,32},{96,64},{128,96},{160,128},{192,160},{224,192},{256... | collective-permute-start | bytes 393224 | tf_op jit(solution)/shard_map/while/body/eval_jaxpr/ppermute | solution.py:21
  341.3 9.5 %collective-permute-start.1 = (f32[2,128,128]{2,1,0:T(8,128)}, f32[2,128,128]{2,1,0:T(8,128)S(1)}, u32[]{:S(2)}, u32[]{:S(2)}) collective-permute-start(f32[2,128,128]{2,1,0:T(8,128)} %multiply_add_fusion.11), channel_id=1, source_target_pairs={{32,0},{64,32},{96,64},{128,96},{160,128},{192,160},{224,192},{256... | collective-permute-start | bytes 393224 | tf_op jit(solution)/shard_map/while/body/eval_jaxpr/ppermute | solution.py:21
  352.2 8.8 %collective-permute-start.1 = (f32[2,128,128]{2,1,0:T(8,128)}, f32[2,128,128]{2,1,0:T(8,128)S(1)}, u32[]{:S(2)}, u32[]{:S(2)}) collective-permute-start(f32[2,128,128]{2,1,0:T(8,128)} %multiply_add_fusion.11), channel_id=1, source_target_pairs={{32,0},{64,32},{96,64},{128,96},{160,128},{192,160},{224,192},{256... | collective-permute-start | bytes 393224 | tf_op jit(solution)/shard_map/while/body/eval_jaxpr/ppermute | solution.py:21
  362.5 8.3 %collective-permute-start.1 = (f32[2,128,128]{2,1,0:T(8,128)}, f32[2,128,128]{2,1,0:T(8,128)S(1)}, u32[]{:S(2)}, u32[]{:S(2)}) collective-permute-start(f32[2,128,128]{2,1,0:T(8,128)} %multiply_add_fusion.11), channel_id=1, source_target_pairs={{32,0},{64,32},{96,64},{128,96},{160,128},{192,160},{224,192},{256... | collective-permute-start | bytes 393224 | tf_op jit(solution)/shard_map/while/body/eval_jaxpr/ppermute | solution.py:21
  372.2 8.3 %collective-permute-start.1 = (f32[2,128,128]{2,1,0:T(8,128)}, f32[2,128,128]{2,1,0:T(8,128)S(1)}, u32[]{:S(2)}, u32[]{:S(2)}) collective-permute-start(f32[2,128,128]{2,1,0:T(8,128)} %multiply_add_fusion.11), channel_id=1, source_target_pairs={{32,0},{64,32},{96,64},{128,96},{160,128},{192,160},{224,192},{256... | collective-permute-start | bytes 393224 | tf_op jit(solution)/shard_map/while/body/eval_jaxpr/ppermute | solution.py:21
  381.8 8.3 %collective-permute-start.1 = (f32[2,128,128]{2,1,0:T(8,128)}, f32[2,128,128]{2,1,0:T(8,128)S(1)}, u32[]{:S(2)}, u32[]{:S(2)}) collective-permute-start(f32[2,128,128]{2,1,0:T(8,128)} %multiply_add_fusion.11), channel_id=1, source_target_pairs={{32,0},{64,32},{96,64},{128,96},{160,128},{192,160},{224,192},{256... | collective-permute-start | bytes 393224 | tf_op jit(solution)/shard_map/while/body/eval_jaxpr/ppermute | solution.py:21
  391.5 8.3 %collective-permute-start.1 = (f32[2,128,128]{2,1,0:T(8,128)}, f32[2,128,128]{2,1,0:T(8,128)S(1)}, u32[]{:S(2)}, u32[]{:S(2)}) collective-permute-start(f32[2,128,128]{2,1,0:T(8,128)} %multiply_add_fusion.11), channel_id=1, source_target_pairs={{32,0},{64,32},{96,64},{128,96},{160,128},{192,160},{224,192},{256... | collective-permute-start | bytes 393224 | tf_op jit(solution)/shard_map/while/body/eval_jaxpr/ppermute | solution.py:21
  401.2 8.3 %collective-permute-start.1 = (f32[2,128,128]{2,1,0:T(8,128)}, f32[2,128,128]{2,1,0:T(8,128)S(1)}, u32[]{:S(2)}, u32[]{:S(2)}) collective-permute-start(f32[2,128,128]{2,1,0:T(8,128)} %multiply_add_fusion.11), channel_id=1, source_target_pairs={{32,0},{64,32},{96,64},{128,96},{160,128},{192,160},{224,192},{256... | collective-permute-start | bytes 393224 | tf_op jit(solution)/shard_map/while/body/eval_jaxpr/ppermute | solution.py:21
  410.9 8.3 %collective-permute-start.1 = (f32[2,128,128]{2,1,0:T(8,128)}, f32[2,128,128]{2,1,0:T(8,128)S(1)}, u32[]{:S(2)}, u32[]{:S(2)}) collective-permute-start(f32[2,128,128]{2,1,0:T(8,128)} %multiply_add_fusion.11), channel_id=1, source_target_pairs={{32,0},{64,32},{96,64},{128,96},{160,128},{192,160},{224,192},{256... | collective-permute-start | bytes 393224 | tf_op jit(solution)/shard_map/while/body/eval_jaxpr/ppermute | solution.py:21
  (31 other events, 852.4 us)
